TPU v7x, 32 devices: a whole 2x2x4 slice. The times are simulated.
32 devices in a mesh: batch: 2 (over x), ctx: 16 (over z, y, core).
Axes of the slice: x: 2, y: 2, z: 4, core: 2. Of those that a mesh axis runs over, the one named last changes fastest.
Arguments:
- inputs: float32 [4, 1024, 768], P('batch', 'ctx'), may hold values from -6 to 6
- teacher: float32 [4, 1024, 768], P('batch', 'ctx'), may hold values from -6 to 6
- segments: int32 [4, 1024], P('batch'), may hold values from 0 to 15, never falling along the last dimension, each value on 1 to 768 neighbouring positions
- w_query: bfloat16 [768, 768], P('batch'), may hold values from -0.21875 to 0.21875
- b_query: bfloat16 [768], P('batch'), may hold values from -4 to 4
- w_key: bfloat16 [768, 768], P('batch'), may hold values from -0.21875 to 0.21875
- w_value: bfloat16 [768, 768], P('batch'), may hold values from -0.21875 to 0.21875
- b_value: bfloat16 [768], P('batch'), may hold values from -0.75 to 0.75
- w_out: bfloat16 [768, 768], P('batch'), may hold values from -1.25 to 1.25
- b_out: bfloat16 [768], P('batch'), may hold values from -4 to 4
- gain_one: bfloat16 [768], P('batch'), may hold values from 0.25 to 1.75
- shift_one: bfloat16 [768], P('batch'), may hold values from -4 to 4
- w_inner: bfloat16 [768, 3072], P('batch'), may hold values from -0.21875 to 0.21875
- b_inner: bfloat16 [3072], P('batch'), may hold values from -4 to 4
- w_outer: bfloat16 [3072, 768], P('batch'), may hold values from -0.109375 to 0.109375
- b_outer: bfloat16 [768], P('batch'), may hold values from -4 to 4
- gain_two: bfloat16 [768], P('batch'), may hold values from 0.25 to 1.75
- shift_two: bfloat16 [768], P('batch'), may hold values from -4 to 4
Outputs:
- output: float32 [4, 1024, 768], P('batch', 'ctx')
- loss: float32 [], replicated
- grad_inputs: float32 [4, 1024, 768], P('batch', 'ctx')
- grad_w_query: float32 [768, 768], P('batch')
- grad_b_query: float32 [768], P('batch')
- grad_w_key: float32 [768, 768], P('batch')
- grad_w_value: float32 [768, 768], P('batch')
- grad_b_value: float32 [768], P('batch')
- grad_w_out: float32 [768, 768], P('batch')
- grad_b_out: float32 [768], P('batch')
- grad_gain_one: float32 [768], P('batch')
- grad_shift_one: float32 [768], P('batch')
- grad_w_inner: float32 [768, 3072], P('batch')
- grad_b_inner: float32 [3072], P('batch')
- grad_w_outer: float32 [3072, 768], P('batch')
- grad_b_outer: float32 [768], P('batch')
- grad_gain_two: float32 [768], P('batch')
- grad_shift_two: float32 [768], P('batch')
Inputs may be any that keep to these rules, and one draw needn't show every extreme that they name: `segments`: segment ids never fall along a sequence, every id of 0 to 15 occurs in each sequence, each segment covers 1 to 768 positions and one covers exactly 768.
All inputs are finite; a program needn't handle non-finite values.
Results may differ from a plain program's by a relative error of at most 0.014.
The roundings to bfloat16 on the way count: a program that leaves them out, or rounds other values in their place, can miss the bound.
Values may be sent and summed in bfloat16 or wider, within the bound.
No kernel may reach another device: no remote copies, remote signals or barrier semaphores. Data moves between devices by JAX's collectives and lax.ppermute only.
A program may use at most 320 MiB of HBM per device.

v0:
```python
import jax
import jax.numpy as jnp
from jax import lax
from jax.sharding import PartitionSpec as P

H = 12
HD = 64
NEGATIVE = -1e30
EPSILON = 1e-12


def norm_rows(hidden, gain, shift):
    center = hidden - jnp.mean(hidden, -1, keepdims=True)
    spread = jnp.mean(center * center, -1, keepdims=True)
    return center * lax.rsqrt(spread + EPSILON) * gain + shift


def gelu_exact(values):
    return jax.nn.gelu(values, approximate=False)


def linear(rows_in, weight):
    return jnp.dot(rows_in, weight, preferred_element_type=jnp.float32)


def contract_rows(left, right):
    return lax.dot_general(
        left, right, (((0,), (0,)), ((), ())), preferred_element_type=jnp.float32
    )


def times_transpose(rows_in, weight):
    return lax.dot_general(
        rows_in, weight, (((1,), (1,)), ((), ())), preferred_element_type=jnp.float32
    )


def score_rows(query_one, keys_all, seg_mine, seg_all):
    heads_query = query_one.reshape(query_one.shape[0], H, HD)
    heads_key = keys_all.reshape(keys_all.shape[0], H, HD)
    raw = jnp.einsum(
        "chd,khd->hck", heads_query, heads_key, preferred_element_type=jnp.float32
    ) * HD ** (-0.5)
    allowed = seg_mine[None, :, None] == seg_all[None, None, :]
    return jnp.where(allowed, raw, NEGATIVE)


def per_device(
    inputs,
    teacher,
    segments,
    w_query,
    b_query,
    w_key,
    w_value,
    b_value,
    w_out,
    b_out,
    gain_one,
    shift_one,
    w_inner,
    b_inner,
    w_outer,
    b_outer,
    gain_two,
    shift_two,
):
    (
        w_query,
        b_query,
        w_key,
        w_value,
        b_value,
        w_out,
        b_out,
        gain_one,
        shift_one,
        w_inner,
        b_inner,
        w_outer,
        b_outer,
        gain_two,
        shift_two,
    ) = (
        lax.all_gather(w_query, "batch", axis=0, tiled=True),
        lax.all_gather(b_query, "batch", axis=0, tiled=True),
        lax.all_gather(w_key, "batch", axis=0, tiled=True),
        lax.all_gather(w_value, "batch", axis=0, tiled=True),
        lax.all_gather(b_value, "batch", axis=0, tiled=True),
        lax.all_gather(w_out, "batch", axis=0, tiled=True),
        lax.all_gather(b_out, "batch", axis=0, tiled=True),
        lax.all_gather(gain_one, "batch", axis=0, tiled=True),
        lax.all_gather(shift_one, "batch", axis=0, tiled=True),
        lax.all_gather(w_inner, "batch", axis=0, tiled=True),
        lax.all_gather(b_inner, "batch", axis=0, tiled=True),
        lax.all_gather(w_outer, "batch", axis=0, tiled=True),
        lax.all_gather(b_outer, "batch", axis=0, tiled=True),
        lax.all_gather(gain_two, "batch", axis=0, tiled=True),
        lax.all_gather(shift_two, "batch", axis=0, tiled=True),
    )
    scale = HD ** (-0.5)
    seqs_here, ctx_rows, width = inputs.shape
    rows_here = seqs_here * ctx_rows
    tokens_all = rows_here * lax.axis_size("batch") * lax.axis_size("ctx")
    seg_own = lax.dynamic_slice_in_dim(segments, lax.axis_index("ctx") * ctx_rows, ctx_rows, 1)
    inputs_flat = inputs.reshape(rows_here, width)
    inputs_low = inputs_flat.astype(jnp.bfloat16)
    query = (linear(inputs_low, w_query) + b_query.astype(jnp.float32)).astype(jnp.bfloat16)
    key = linear(inputs_low, w_key).astype(jnp.bfloat16)
    value = (linear(inputs_low, w_value) + b_value.astype(jnp.float32)).astype(jnp.bfloat16)
    query_seq = query.reshape(seqs_here, ctx_rows, width)
    key_seq = key.reshape(seqs_here, ctx_rows, width)
    value_seq = value.reshape(seqs_here, ctx_rows, width)

    def attend_forward(items):
        query_one, key_one, value_one, seg_all, seg_mine = items
        keys_all, values_all = (
            lax.all_gather(key_one, "ctx", axis=0, tiled=True),
            lax.all_gather(value_one, "ctx", axis=0, tiled=True),
        )
        scores = score_rows(query_one, keys_all, seg_mine, seg_all)
        highest = jnp.max(scores, -1, keepdims=True)
        expo = jnp.exp(scores - highest)
        totals = jnp.sum(expo, -1, keepdims=True)
        probs = (expo / totals).astype(jnp.bfloat16)
        mixed = jnp.einsum(
            "hck,khd->chd",
            probs,
            values_all.reshape(keys_all.shape[0], H, HD),
            preferred_element_type=jnp.float32,
        )
        return (
            mixed.reshape(ctx_rows, width).astype(jnp.bfloat16),
            (highest + jnp.log(totals))[:, :, 0],
        )

    attended, log_totals = lax.map(
        attend_forward, (query_seq, key_seq, value_seq, segments, seg_own)
    )
    attended_flat = attended.reshape(rows_here, width)
    gain_one_full = gain_one.astype(jnp.float32)
    shift_one_full = shift_one.astype(jnp.float32)
    gain_two_full = gain_two.astype(jnp.float32)
    shift_two_full = shift_two.astype(jnp.float32)
    hidden_one = inputs_flat + linear(attended_flat, w_out) + b_out.astype(jnp.float32)
    normed_one, back_one = jax.vjp(norm_rows, hidden_one, gain_one_full, shift_one_full)
    normed_low = normed_one.astype(jnp.bfloat16)
    inner_pre = linear(normed_low, w_inner) + b_inner.astype(jnp.float32)
    active_full, gelu_back = jax.vjp(gelu_exact, inner_pre)
    active_low = active_full.astype(jnp.bfloat16)
    hidden_two = normed_one + linear(active_low, w_outer) + b_outer.astype(jnp.float32)
    output, back_two = jax.vjp(norm_rows, hidden_two, gain_two_full, shift_two_full)
    valid = (seg_own.reshape(rows_here) != 0).astype(jnp.float32)[:, None]
    error = output - teacher.reshape(rows_here, width)
    loss_total, valid_count = lax.psum(
        (jnp.sum(valid * error * error), jnp.sum(valid)), ("batch", "ctx")
    )
    loss = loss_total / (2.0 * valid_count)
    grad_output = tokens_all / valid_count * valid * error
    grad_hidden_two, grad_gain_two, grad_shift_two = back_two(grad_output)
    grad_branch_two = grad_hidden_two.astype(jnp.bfloat16)
    grad_b_outer = jnp.sum(grad_branch_two.astype(jnp.float32), 0)
    grad_w_outer = contract_rows(active_low, grad_branch_two)
    grad_active = times_transpose(grad_branch_two, w_outer)
    grad_inner = gelu_back(grad_active)[0].astype(jnp.bfloat16)
    grad_b_inner = jnp.sum(grad_inner.astype(jnp.float32), 0)
    grad_w_inner = contract_rows(normed_low, grad_inner)
    grad_normed = grad_hidden_two + times_transpose(grad_inner, w_inner)
    grad_hidden_one, grad_gain_one, grad_shift_one = back_one(grad_normed)
    grad_branch_one = grad_hidden_one.astype(jnp.bfloat16)
    grad_b_out = jnp.sum(grad_branch_one.astype(jnp.float32), 0)
    grad_w_out = contract_rows(attended_flat, grad_branch_one)
    grad_attended = (
        times_transpose(grad_branch_one, w_out)
        .astype(jnp.bfloat16)
        .reshape(seqs_here, ctx_rows, width)
    )

    def attend_backward(items):
        query_one, key_one, value_one, seg_all, seg_mine, log_one, grad_one = items
        keys_all, values_all = (
            lax.all_gather(key_one, "ctx", axis=0, tiled=True),
            lax.all_gather(value_one, "ctx", axis=0, tiled=True),
        )
        key_count = keys_all.shape[0]
        scores = score_rows(query_one, keys_all, seg_mine, seg_all)
        probs = jnp.exp(scores - log_one[:, :, None])
        grad_heads = grad_one.reshape(ctx_rows, H, HD)
        grad_probs = jnp.einsum(
            "chd,khd->hck",
            grad_heads,
            values_all.reshape(key_count, H, HD),
            preferred_element_type=jnp.float32,
        )
        centre = jnp.sum(probs * grad_probs, -1)
        grad_scores = (probs * (grad_probs - centre[:, :, None])).astype(jnp.bfloat16)
        grad_query = (
            jnp.einsum(
                "hck,khd->chd",
                grad_scores,
                keys_all.reshape(key_count, H, HD),
                preferred_element_type=jnp.float32,
            )
            * scale
        )
        grad_query = grad_query.reshape(ctx_rows, width).astype(jnp.bfloat16)
        probs_low = probs.astype(jnp.bfloat16)
        query_heads = query_one.reshape(ctx_rows, H, HD)
        count = ctx_rows * lax.axis_size("ctx")
        grad_key = (
            jnp.einsum("hck,chd->khd", grad_scores, query_heads, preferred_element_type=jnp.float32)
            * scale
        )
        grad_value = jnp.einsum(
            "hck,chd->khd", probs_low, grad_heads, preferred_element_type=jnp.float32
        )
        both = lax.psum_scatter(
            jnp.concatenate([grad_key.reshape(count, width), grad_value.reshape(count, width)], 1),
            "ctx",
            scatter_dimension=0,
            tiled=True,
        )
        return (
            grad_query,
            both[:, :width].astype(jnp.bfloat16),
            both[:, width:].astype(jnp.bfloat16),
        )

    grad_query_seq, grad_key_seq, grad_value_seq = lax.map(
        attend_backward,
        (query_seq, key_seq, value_seq, segments, seg_own, log_totals, grad_attended),
    )
    grad_query_flat = grad_query_seq.reshape(rows_here, width)
    grad_key_flat = grad_key_seq.reshape(rows_here, width)
    grad_value_flat = grad_value_seq.reshape(rows_here, width)
    grad_w_query = contract_rows(inputs_low, grad_query_flat)
    grad_b_query = jnp.sum(grad_query_flat.astype(jnp.float32), 0)
    grad_w_key = contract_rows(inputs_low, grad_key_flat)
    grad_w_value = contract_rows(inputs_low, grad_value_flat)
    grad_b_value = jnp.sum(grad_value_flat.astype(jnp.float32), 0)
    grad_inputs = (
        grad_hidden_one
        + times_transpose(grad_query_flat, w_query)
        + times_transpose(grad_key_flat, w_key)
        + times_transpose(grad_value_flat, w_value)
    )
    (
        grad_w_query,
        grad_b_query,
        grad_w_key,
        grad_w_value,
        grad_b_value,
        grad_w_out,
        grad_b_out,
        grad_gain_one,
        grad_shift_one,
        grad_w_inner,
        grad_b_inner,
        grad_w_outer,
        grad_b_outer,
        grad_gain_two,
        grad_shift_two,
    ) = (
        lax.psum_scatter(
            grad_w_query.astype(jnp.bfloat16), "batch", scatter_dimension=0, tiled=True
        ).astype(jnp.float32),
        lax.psum_scatter(
            grad_b_query.astype(jnp.bfloat16), "batch", scatter_dimension=0, tiled=True
        ).astype(jnp.float32),
        lax.psum_scatter(
            grad_w_key.astype(jnp.bfloat16), "batch", scatter_dimension=0, tiled=True
        ).astype(jnp.float32),
        lax.psum_scatter(
            grad_w_value.astype(jnp.bfloat16), "batch", scatter_dimension=0, tiled=True
        ).astype(jnp.float32),
        lax.psum_scatter(
            grad_b_value.astype(jnp.bfloat16), "batch", scatter_dimension=0, tiled=True
        ).astype(jnp.float32),
        lax.psum_scatter(
            grad_w_out.astype(jnp.bfloat16), "batch", scatter_dimension=0, tiled=True
        ).astype(jnp.float32),
        lax.psum_scatter(
            grad_b_out.astype(jnp.bfloat16), "batch", scatter_dimension=0, tiled=True
        ).astype(jnp.float32),
        lax.psum_scatter(
            grad_gain_one.astype(jnp.bfloat16), "batch", scatter_dimension=0, tiled=True
        ).astype(jnp.float32),
        lax.psum_scatter(
            grad_shift_one.astype(jnp.bfloat16), "batch", scatter_dimension=0, tiled=True
        ).astype(jnp.float32),
        lax.psum_scatter(
            grad_w_inner.astype(jnp.bfloat16), "batch", scatter_dimension=0, tiled=True
        ).astype(jnp.float32),
        lax.psum_scatter(
            grad_b_inner.astype(jnp.bfloat16), "batch", scatter_dimension=0, tiled=True
        ).astype(jnp.float32),
        lax.psum_scatter(
            grad_w_outer.astype(jnp.bfloat16), "batch", scatter_dimension=0, tiled=True
        ).astype(jnp.float32),
        lax.psum_scatter(
            grad_b_outer.astype(jnp.bfloat16), "batch", scatter_dimension=0, tiled=True
        ).astype(jnp.float32),
        lax.psum_scatter(
            grad_gain_two.astype(jnp.bfloat16), "batch", scatter_dimension=0, tiled=True
        ).astype(jnp.float32),
        lax.psum_scatter(
            grad_shift_two.astype(jnp.bfloat16), "batch", scatter_dimension=0, tiled=True
        ).astype(jnp.float32),
    )
    (
        grad_w_query,
        grad_b_query,
        grad_w_key,
        grad_w_value,
        grad_b_value,
        grad_w_out,
        grad_b_out,
        grad_gain_one,
        grad_shift_one,
        grad_w_inner,
        grad_b_inner,
        grad_w_outer,
        grad_b_outer,
        grad_gain_two,
        grad_shift_two,
    ) = lax.psum(
        (
            grad_w_query,
            grad_b_query,
            grad_w_key,
            grad_w_value,
            grad_b_value,
            grad_w_out,
            grad_b_out,
            grad_gain_one,
            grad_shift_one,
            grad_w_inner,
            grad_b_inner,
            grad_w_outer,
            grad_b_outer,
            grad_gain_two,
            grad_shift_two,
        ),
        "ctx",
    )
    return (
        output.reshape(inputs.shape),
        loss,
        grad_inputs.reshape(inputs.shape),
        grad_w_query,
        grad_b_query,
        grad_w_key,
        grad_w_value,
        grad_b_value,
        grad_w_out,
        grad_b_out,
        grad_gain_one,
        grad_shift_one,
        grad_w_inner,
        grad_b_inner,
        grad_w_outer,
        grad_b_outer,
        grad_gain_two,
        grad_shift_two,
    )


def solution(mesh):
    placed = (
        P("batch", "ctx", None),
        P("batch", "ctx", None),
        P("batch", None),
        P("batch", None),
        P("batch"),
        P("batch", None),
        P("batch", None),
        P("batch"),
        P("batch", None),
        P("batch"),
        P("batch"),
        P("batch"),
        P("batch", None),
        P("batch"),
        P("batch", None),
        P("batch"),
        P("batch"),
        P("batch"),
    )
    return jax.shard_map(
        per_device,
        mesh=mesh,
        in_specs=placed,
        out_specs=(
            P("batch", "ctx", None),
            P(),
            P("batch", "ctx", None),
            P("batch", None),
            P("batch"),
            P("batch", None),
            P("batch", None),
            P("batch"),
            P("batch", None),
            P("batch"),
            P("batch"),
            P("batch"),
            P("batch", None),
            P("batch"),
            P("batch", None),
            P("batch"),
            P("batch"),
            P("batch"),
        ),
        check_vma=False,
    )
```

profile of v0, /device:TPU:1, one launch (start us, length us, event | category | flops | bytes accessed | tf_op | source)
XLA Modules:
  0.0 1352.9 jit_solution(5243858806981145889)
XLA Ops:
  9.5 3.7 all-gather.5
  13.3 3.2 all-gather.4
  17.3 17.2 %all-gather.36.cloned.1.call-done = bf16[768,768]{1,0:T(8,128)(2,1)} async-done(((bf16[384,768]{1,0:T(8,128)(2,1)}), bf16[768,768]{1,0:T(8,128)(2,1)}) %all-gather.36.cloned.1.call-update) | async-done | bytes 1179664 | tf_op jit(solution)/shard_map/all_gather | solution.py:87
  36.8 22.1 %all-gather.34.cloned.1.call-done = bf16[768,768]{1,0:T(8,128)(2,1)} async-done(((bf16[384,768]{1,0:T(8,128)(2,1)}), bf16[768,768]{1,0:T(8,128)(2,1)}) %all-gather.34.cloned.1.call-update) | async-done | bytes 1179664 | tf_op jit(solution)/shard_map/all_gather | solution.py:85
  61.1 22.1 %all-gather.32.cloned.1.call-done = bf16[768,768]{1,0:T(8,128)(2,1)} async-done(((bf16[384,768]{1,0:T(8,128)(2,1)}), bf16[768,768]{1,0:T(8,128)(2,1)}) %all-gather.32.cloned.1.call-update) | async-done | bytes 1179664 | tf_op jit(solution)/shard_map/all_gather | solution.py:88
  85.5 181.2 %while.26 = (s32[]{:T(128)}, bf16[2,64,768]{2,1,0:T(8,128)(2,1)}, f32[2,12,64]{2,1,0:T(8,128)}, bf16[2,64,768]{2,1,0:T(8,128)(2,1)}, s32[2,64]{1,0:T(2,128)S(1)}...) while((s32[]{:T(128)}, bf16[2,64,768]{2,1,0:T(8,128)(2,1)}, ...), condition=%wide.region_3.4_spmd, body=%wide.region_0.3_spmd.sunk | while | flops 210877696 | bytes 30582736 | solution.py:137
  90.6 38.4 %all-gather.46.cloned.1.call-done = bf16[1,1024,768]{2,1,0:T(8,128)(2,1)} async-done(((bf16[1,64,768]{2,1,0:T(8,128)(2,1)}), bf16[1,1024,768]{2,1,0:T(8,128)(2,1)}) %all-gather.46.cloned.1.call-update) | async-done | bytes 1572880 | tf_op jit(solution)/shard_map/while/body/eval_jaxpr/all_gather | solution.py:118
  129.0 2.6 copy.122
  134.6 35.7 %all-gather.44.cloned.1.call-done = bf16[1,1024,768]{2,1,0:T(8,128)(2,1)} async-done(((bf16[1,64,768]{2,1,0:T(8,128)(2,1)}), bf16[1,1024,768]{2,1,0:T(8,128)(2,1)}) %all-gather.44.cloned.1.call-update) | async-done | bytes 1572880 | tf_op jit(solution)/shard_map/while/body/eval_jaxpr/all_gather | solution.py:119
  181.9 36.9 %all-gather.46.cloned.1.call-done = bf16[1,1024,768]{2,1,0:T(8,128)(2,1)} async-done(((bf16[1,64,768]{2,1,0:T(8,128)(2,1)}), bf16[1,1024,768]{2,1,0:T(8,128)(2,1)}) %all-gather.46.cloned.1.call-update) | async-done | bytes 1572880 | tf_op jit(solution)/shard_map/while/body/eval_jaxpr/all_gather | solution.py:118
  224.4 35.8 %all-gather.44.cloned.1.call-done = bf16[1,1024,768]{2,1,0:T(8,128)(2,1)} async-done(((bf16[1,64,768]{2,1,0:T(8,128)(2,1)}), bf16[1,1024,768]{2,1,0:T(8,128)(2,1)}) %all-gather.44.cloned.1.call-update) | async-done | bytes 1572880 | tf_op jit(solution)/shard_map/while/body/eval_jaxpr/all_gather | solution.py:119
  260.2 2.6 copy.121
  269.5 38.7 %psum.120 = f32[]{:T(128)} all-reduce(f32[]{:T(128)} %convert_reduce_fusion.8), channel_id=1, replica_groups=mesh['batch'=2,'ctx'=16] {'batch','ctx'}, use_global_device_ids=true, to_apply=%region_11.12 | all-reduce | flops 1 | bytes 8 | tf_op jit(solution)/shard_map/psum | solution.py:155
  308.2 3.5 all-gather.6
  311.8 3.5 all-gather.7
  315.3 3.5 all-gather.8
  318.9 3.5 all-gather.10
  322.5 3.5 all-gather.11
  326.0 3.5 all-gather.12
  330.4 3.8 all-gather.9
  336.3 19.3 %all-gather.40.cloned.1.call-done = bf16[768,3072]{1,0:T(8,128)(2,1)} async-done(((bf16[384,3072]{1,0:T(8,128)(2,1)}), bf16[768,3072]{1,0:T(8,128)(2,1)}) %all-gather.40.cloned.1.call-update) | async-done | bytes 4718608 | tf_op jit(solution)/shard_map/all_gather | solution.py:94
  355.6 7.6 multiply_convert_fusion.1
  363.2 56.3 %all-gather.42.cloned.1.call-done = bf16[3072,768]{1,0:T(8,128)(2,1)} async-done(((bf16[1536,768]{1,0:T(8,128)(2,1)}), bf16[3072,768]{1,0:T(8,128)(2,1)}) %all-gather.42.cloned.1.call-update) | async-done | bytes 4718608 | tf_op jit(solution)/shard_map/all_gather | solution.py:96
  419.5 3.4 fusion.45
  433.6 376.0 %while.27 = (s32[]{:T(128)}, bf16[2,64,768]{1,2,0:T(8,128)(2,1)}, bf16[2,64,768]{1,2,0:T(8,128)(2,1)}, bf16[2,64,768]{1,2,0:T(8,128)(2,1)}, bf16[2,64,768]{2,1,0...) while((s32[]{:T(128)}, bf16[2,64,768]{1,2,0:T(8,128)(2,1)}, ...), condition=%wide.region_19.20_spmd, body=%wide.region_16.19_spmd.sunk | while | flops 512916736 | bytes 120094944 | solution.py:229
  440.3 37.1 %all-gather.50.cloned.1.call-done = bf16[1,1024,768]{2,1,0:T(8,128)(2,1)} async-done(((bf16[1,64,768]{2,1,0:T(8,128)(2,1)}), bf16[1,1024,768]{2,1,0:T(8,128)(2,1)}) %all-gather.50.cloned.1.call-update) | async-done | bytes 1572880 | tf_op jit(solution)/shard_map/while/body/eval_jaxpr/all_gather | solution.py:183
  482.0 36.7 %all-gather.48.cloned.1.call-done = bf16[1,1024,768]{2,1,0:T(8,128)(2,1)} async-done(((bf16[1,64,768]{2,1,0:T(8,128)(2,1)}), bf16[1,1024,768]{2,1,0:T(8,128)(2,1)}) %all-gather.48.cloned.1.call-update) | async-done | bytes 1572880 | tf_op jit(solution)/shard_map/while/body/eval_jaxpr/all_gather | solution.py:182
  518.7 2.6 copy.124
  521.3 2.8 multiply_reduce_fusion.9
  526.1 3.2 pad_maximum_fusion.2
  529.4 6.6 copy.128
  539.1 80.0 %reduce-scatter.30.cloned.1.call-done = f32[64,1536]{1,0:T(8,128)} async-done(((f32[1024,1536]{1,0:T(8,128)}), f32[64,1536]{1,0:T(8,128)}) %reduce-scatter.30.cloned.1.call-update) | async-done | bytes 393232 | tf_op jit(solution)/shard_map/while
  628.5 36.6 %all-gather.50.cloned.1.call-done = bf16[1,1024,768]{2,1,0:T(8,128)(2,1)} async-done(((bf16[1,64,768]{2,1,0:T(8,128)(2,1)}), bf16[1,1024,768]{2,1,0:T(8,128)(2,1)}) %all-gather.50.cloned.1.call-update) | async-done | bytes 1572880 | tf_op jit(solution)/shard_map/while/body/eval_jaxpr/all_gather | solution.py:183
  665.2 2.6 copy.126
  669.8 36.7 %all-gather.48.cloned.1.call-done = bf16[1,1024,768]{2,1,0:T(8,128)(2,1)} async-done(((bf16[1,64,768]{2,1,0:T(8,128)(2,1)}), bf16[1,1024,768]{2,1,0:T(8,128)(2,1)}) %all-gather.48.cloned.1.call-update) | async-done | bytes 1572880 | tf_op jit(solution)/shard_map/while/body/eval_jaxpr/all_gather | solution.py:182
  709.0 2.8 multiply_reduce_fusion.9
  713.9 3.2 pad_maximum_fusion.2
  717.1 6.6 copy.128
  726.9 80.0 %reduce-scatter.30.cloned.1.call-done = f32[64,1536]{1,0:T(8,128)} async-done(((f32[1024,1536]{1,0:T(8,128)}), f32[64,1536]{1,0:T(8,128)}) %reduce-scatter.30.cloned.1.call-update) | async-done | bytes 393232 | tf_op jit(solution)/shard_map/while
  818.6 3.7 convolution_convert_fusion.1
  823.4 3.6 convolution_convert_fusion
  830.2 39.9 %psum.119 = f32[]{:T(128)} all-reduce(f32[]{:T(128)} %get-tuple-element.222), channel_id=1, replica_groups=mesh['batch'=2,'ctx'=16] {'batch','ctx'}, use_global_device_ids=true, to_apply=%region_9.10 | all-reduce | flops 1 | bytes 8 | tf_op jit(solution)/shard_map/psum | solution.py:155
  875.7 7.7 all-reduce.10
  891.6 17.3 %reduce-scatter.18.cloned.1.call-done = bf16[384,768]{1,0:T(8,128)(2,1)} async-done(((bf16[768,768]{1,0:T(8,128)(2,1)}), bf16[384,768]{1,0:T(8,128)(2,1)}) %reduce-scatter.18.cloned.1.call-update) | async-done | bytes 589840 | tf_op jit(solution)/shard_map/reduce_scatter | solution.py:279
  908.9 62.9 %reduce-scatter.20.cloned.1.call-done = bf16[384,3072]{1,0:T(8,128)(2,1)} async-done(((bf16[768,3072]{1,0:T(8,128)(2,1)}), bf16[384,3072]{1,0:T(8,128)(2,1)}) %reduce-scatter.20.cloned.1.call-update) | async-done | bytes 2359312 | tf_op jit(solution)/shard_map/reduce_scatter | solution.py:291
  971.8 63.0 %reduce-scatter.22.cloned.1.call-done = bf16[1536,768]{1,0:T(8,128)(2,1)} async-done(((bf16[3072,768]{1,0:T(8,128)(2,1)}), bf16[1536,768]{1,0:T(8,128)(2,1)}) %reduce-scatter.22.cloned.1.call-update) | async-done | bytes 2359312 | tf_op jit(solution)/shard_map/reduce_scatter | solution.py:297
  1034.8 304.6 %all-reduce.12 = (f32[384,768]{0,1:T(8,128)}, f32[384]{0:T(512)}, f32[384,768]{0,1:T(8,128)}, f32[384,768]{0,1:T(8,128)S(1)}, f32[384]{0:T(512)}, /*index=5*/f32...) all-reduce(bf16[384,768]{0,1:T(8,128)(2,1)S(1)} %copy.92, ...), channel_id=1, replica_groups=mesh['batch'=2,'ctx'=16] {'ctx'}, use_global_device_ids=true, to_apply=%region_21.22 | all-reduce | flops 3543552 | bytes 21270528 | tf_op jit(solution)/shard_map/psum | solution.py:326
  1339.4 2.7 copy.83
  (324 shorter events, 119.8 us)
Async XLA Ops:
  7.2 10.0 copy-start.5
  7.2 27.3 %all-gather.36.cloned.1.call-start = ((), (), s32[]{:S(2)}) async-start(), calls=%async_computation.9 | async-start | bytes 1769472 | tf_op jit(solution)/shard_map/all_gather | solution.py:87
  8.0 50.9 %all-gather.34.cloned.1.call-start = ((), (), s32[]{:S(2)}) async-start(), calls=%async_computation.8 | async-start | bytes 1769472 | tf_op jit(solution)/shard_map/all_gather | solution.py:85
  8.7 74.5 %all-gather.32.cloned.1.call-start = ((), (), s32[]{:S(2)}) async-start(), calls=%async_computation.7 | async-start | bytes 1769472 | tf_op jit(solution)/shard_map/all_gather | solution.py:88
  85.5 43.5 %all-gather.46.cloned.1.call-start = ((), (), s32[]{:S(2)}) async-start(), calls=%async_computation.20 | async-start | bytes 1671168 | tf_op jit(solution)/shard_map/while/body/eval_jaxpr/all_gather | solution.py:118
  87.1 83.2 %all-gather.44.cloned.1.call-start = ((), (), s32[]{:S(2)}) async-start(), calls=%async_computation.19 | async-start | bytes 1671168 | tf_op jit(solution)/shard_map/while/body/eval_jaxpr/all_gather | solution.py:119
  176.8 42.0 %all-gather.46.cloned.1.call-start = ((), (), s32[]{:S(2)}) async-start(), calls=%async_computation.20 | async-start | bytes 1671168 | tf_op jit(solution)/shard_map/while/body/eval_jaxpr/all_gather | solution.py:118
  178.3 81.8 %all-gather.44.cloned.1.call-start = ((), (), s32[]{:S(2)}) async-start(), calls=%async_computation.19 | async-start | bytes 1671168 | tf_op jit(solution)/shard_map/while/body/eval_jaxpr/all_gather | solution.py:119
  266.7 67.6 %all-gather.38.cloned.1.call-start = ((), (), s32[]{:S(2)}) async-start(), calls=%async_computation.10 | async-start | bytes 1769472 | tf_op jit(solution)/shard_map/all_gather | solution.py:90
  267.4 88.2 %all-gather.40.cloned.1.call-start = ((), (), s32[]{:S(2)}) async-start(), calls=%async_computation.11 | async-start | bytes 7077888 | tf_op jit(solution)/shard_map/all_gather | solution.py:94
  268.2 40.0 %copy-start.46 = (bf16[384]{0:T(512)(128)(2,1)S(1)}, bf16[384]{0:T(512)(128)(2,1)}, u32[]{:S(2)}) copy-start(bf16[384]{0:T(512)(128)(2,1)} %param.31) | copy-start | bytes 2308
  268.2 43.6 %copy-start.47 = (bf16[384]{0:T(512)(128)(2,1)S(1)}, bf16[384]{0:T(512)(128)(2,1)}, u32[]{:S(2)}) copy-start(bf16[384]{0:T(512)(128)(2,1)} %param.32) | copy-start | bytes 2308
  268.2 47.1 %copy-start.48 = (bf16[384]{0:T(512)(128)(2,1)S(1)}, bf16[384]{0:T(512)(128)(2,1)}, u32[]{:S(2)}) copy-start(bf16[384]{0:T(512)(128)(2,1)} %param.33) | copy-start | bytes 2308
  268.2 50.7 %copy-start.49 = (bf16[384]{0:T(512)(128)(2,1)S(1)}, bf16[384]{0:T(512)(128)(2,1)}, u32[]{:S(2)}) copy-start(bf16[384]{0:T(512)(128)(2,1)} %param.37) | copy-start | bytes 2308
  268.2 54.2 %copy-start.50 = (bf16[384]{0:T(512)(128)(2,1)S(1)}, bf16[384]{0:T(512)(128)(2,1)}, u32[]{:S(2)}) copy-start(bf16[384]{0:T(512)(128)(2,1)} %param.38) | copy-start | bytes 2308
  268.2 57.8 %copy-start.51 = (bf16[384]{0:T(512)(128)(2,1)S(1)}, bf16[384]{0:T(512)(128)(2,1)}, u32[]{:S(2)}) copy-start(bf16[384]{0:T(512)(128)(2,1)} %param.39) | copy-start | bytes 2308
  268.2 62.2 %copy-start.42 = (bf16[1536]{0:T(1024)(128)(2,1)S(1)}, bf16[1536]{0:T(1024)(128)(2,1)}, u32[]{:S(2)}) copy-start(bf16[1536]{0:T(1024)(128)(2,1)} %param.35) | copy-start | bytes 9220
  268.2 66.1 %copy-start.6 = (f32[2,64,768]{2,1,0:T(8,128)S(1)}, f32[2,64,768]{2,1,0:T(8,128)}, u32[]{:S(2)}) copy-start(f32[2,64,768]{2,1,0:T(8,128)} %param.22) | copy-start | bytes 1179652
  268.3 66.1 %copy-start.26 = (bf16[2,64,768]{2,1,0:T(8,128)(2,1)S(1)}, bf16[2,64,768]{2,1,0:T(8,128)(2,1)}, u32[]{:S(2)}) copy-start(bf16[2,64,768]{2,1,0:T(8,128)(2,1)} %get-tuple-element.120) | copy-start | bytes 589828
  268.3 151.2 %all-gather.42.cloned.1.call-start = ((), (), s32[]{:S(2)}) async-start(), calls=%async_computation.12 | async-start | bytes 7077888 | tf_op jit(solution)/shard_map/all_gather | solution.py:96
  336.0 94.6 %copy-start.3 = (f32[128,768]{1,0:T(8,128)}, f32[128,768]{1,0:T(8,128)S(1)}, u32[]{:S(2)}) copy-start(f32[128,768]{1,0:T(8,128)S(1)} %get-tuple-element.311) | copy-start | bytes 1179652
  336.0 94.6 %copy-start.32 = (f32[128]{0:T(128)}, f32[128]{0:T(128)S(1)}, u32[]{:S(2)}) copy-start(f32[128]{0:T(128)S(1)} %broadcast_multiply_fusion.1) | copy-start | bytes 1540
  336.3 94.4 %copy-start.34 = (f32[128]{0:T(128)}, f32[128]{0:T(128)S(1)}, u32[]{:S(2)}) copy-start(f32[128]{0:T(128)S(1)} %fusion.30) | copy-start | bytes 1540
  363.2 59.7 %copy-start.8 = (bf16[128,3072]{1,0:T(8,128)(2,1)}, bf16[128,3072]{1,0:T(8,128)(2,1)S(1)}, u32[]{:S(2)}) copy-start(bf16[128,3072]{1,0:T(8,128)(2,1)S(1)} %get-tuple-element.300) | copy-start | bytes 2359300
  433.6 43.8 %all-gather.50.cloned.1.call-start = ((), (), s32[]{:S(2)}) async-start(), calls=%async_computation.22 | async-start | bytes 1671168 | tf_op jit(solution)/shard_map/while/body/eval_jaxpr/all_gather | solution.py:183
  435.2 83.5 %all-gather.48.cloned.1.call-start = ((), (), s32[]{:S(2)}) async-start(), calls=%async_computation.21 | async-start | bytes 1671168 | tf_op jit(solution)/shard_map/while/body/eval_jaxpr/all_gather | solution.py:182
  436.8 182.3 %reduce-scatter.30.cloned.1.call-start = ((), (), s32[]{:S(2)}) async-start(), calls=%async_computation.23 | async-start | bytes 6684672 | tf_op jit(solution)/shard_map/while
  537.8 82.5 %copy-start.17 = (bf16[2,64,768]{1,2,0:T(8,128)(2,1)S(1)}, bf16[2,64,768]{1,2,0:T(8,128)(2,1)}, u32[]{:S(2)}) copy-start(bf16[2,64,768]{1,2,0:T(8,128)(2,1)} %get-tuple-element.498) | copy-start | bytes 589828 | tf_op jit(solution)/shard_map/while
  538.4 83.4 %copy-start.41 = (s32[2,64]{1,0:T(2,128)S(1)}, s32[2,64]{1,0:T(2,128)}, u32[]{:S(2)}) copy-start(s32[2,64]{1,0:T(2,128)} %copy-done.40) | copy-start | bytes 1540 | tf_op jit(solution)/shard_map/while
  621.8 43.3 %all-gather.50.cloned.1.call-start = ((), (), s32[]{:S(2)}) async-start(), calls=%async_computation.22 | async-start | bytes 1671168 | tf_op jit(solution)/shard_map/while/body/eval_jaxpr/all_gather | solution.py:183
  623.4 83.1 %all-gather.48.cloned.1.call-start = ((), (), s32[]{:S(2)}) async-start(), calls=%async_computation.21 | async-start | bytes 1671168 | tf_op jit(solution)/shard_map/while/body/eval_jaxpr/all_gather | solution.py:182
  625.0 181.8 %reduce-scatter.30.cloned.1.call-start = ((), (), s32[]{:S(2)}) async-start(), calls=%async_computation.23 | async-start | bytes 6684672 | tf_op jit(solution)/shard_map/while
  725.6 82.5 %copy-start.17 = (bf16[2,64,768]{1,2,0:T(8,128)(2,1)S(1)}, bf16[2,64,768]{1,2,0:T(8,128)(2,1)}, u32[]{:S(2)}) copy-start(bf16[2,64,768]{1,2,0:T(8,128)(2,1)} %get-tuple-element.498) | copy-start | bytes 589828 | tf_op jit(solution)/shard_map/while
  726.1 83.4 %copy-start.41 = (s32[2,64]{1,0:T(2,128)S(1)}, s32[2,64]{1,0:T(2,128)}, u32[]{:S(2)}) copy-start(s32[2,64]{1,0:T(2,128)} %copy-done.40) | copy-start | bytes 1540 | tf_op jit(solution)/shard_map/while
  809.5 77.9 %reduce-scatter.24.cloned.1.call-start = ((), (), s32[]{:S(2)}) async-start(), calls=%async_computation.16 | async-start | bytes 1769472
  812.7 76.2 %reduce-scatter.28.cloned.1.call-start = ((), (), s32[]{:S(2)}) async-start(), calls=%async_computation.18 | async-start | bytes 1769472
  814.7 75.5 %reduce-scatter.26.cloned.1.call-start = ((), (), s32[]{:S(2)}) async-start(), calls=%async_computation.17 | async-start | bytes 1769472
  816.9 92.0 %reduce-scatter.18.cloned.1.call-start = ((), (), s32[]{:S(2)}) async-start(), calls=%async_computation.13 | async-start | bytes 1769472 | tf_op jit(solution)/shard_map/reduce_scatter | solution.py:279
  818.5 153.4 %reduce-scatter.20.cloned.1.call-start = ((), (), s32[]{:S(2)}) async-start(), calls=%async_computation.14 | async-start | bytes 7077888 | tf_op jit(solution)/shard_map/reduce_scatter | solution.py:291
  822.3 212.6 %reduce-scatter.22.cloned.1.call-start = ((), (), s32[]{:S(2)}) async-start(), calls=%async_computation.15 | async-start | bytes 7077888 | tf_op jit(solution)/shard_map/reduce_scatter | solution.py:297
  827.1 48.6 %copy-start.36 = (bf16[768]{0:T(1024)(128)(2,1)S(1)}, bf16[768]{0:T(1024)(128)(2,1)}, u32[]{:S(2)}) copy-start(bf16[768]{0:T(1024)(128)(2,1)} %get-tuple-element.217) | copy-start | bytes 4612
  827.1 48.6 %copy-start.37 = (bf16[768]{0:T(1024)(128)(2,1)S(1)}, bf16[768]{0:T(1024)(128)(2,1)}, u32[]{:S(2)}) copy-start(bf16[768]{0:T(1024)(128)(2,1)} %get-tuple-element.221) | copy-start | bytes 4612
  827.1 48.6 %copy-start.38 = (bf16[768]{0:T(1024)(128)(2,1)S(1)}, bf16[768]{0:T(1024)(128)(2,1)}, u32[]{:S(2)}) copy-start(bf16[768]{0:T(1024)(128)(2,1)} %get-tuple-element.286) | copy-start | bytes 4612
  827.1 48.6 %copy-start.39 = (bf16[768]{0:T(1024)(128)(2,1)S(1)}, bf16[768]{0:T(1024)(128)(2,1)}, u32[]{:S(2)}) copy-start(bf16[768]{0:T(1024)(128)(2,1)} %get-tuple-element.219) | copy-start | bytes 4612
  827.1 56.7 %copy-start.13 = (bf16[768,768]{1,0:T(8,128)(2,1)S(1)}, bf16[768,768]{1,0:T(8,128)(2,1)}, u32[]{:S(2)}) copy-start(bf16[768,768]{1,0:T(8,128)(2,1)} %all-gather.34.cloned.1.call-done) | copy-start | bytes 3538948
  827.1 56.6 %copy-start.16 = (f32[128,768]{1,0:T(8,128)S(1)}, f32[128,768]{1,0:T(8,128)}, u32[]{:S(2)}) copy-start(f32[128,768]{1,0:T(8,128)} %copy-done.15) | copy-start | bytes 1179652
  873.7 11.2 copy-start.11
  873.7 11.2 copy-start.28
  (37 other events, 80.6 us)
Sparse Core Ops, SparseCore 0:
  9.6 24.8 all-gather.35
  36.0 22.7 all-gather.33
  60.4 22.7 all-gather.31
  88.9 40.0 all-gather.45
  131.7 38.5 all-gather.43
  180.1 38.5 all-gather.45
  221.6 38.5 all-gather.43
  269.1 21.3 all-gather.37
  292.0 63.5 all-gather.39
  357.0 62.4 all-gather.41
  437.3 40.1 all-gather.49
  480.1 38.5 all-gather.47
  536.1 82.9 reduce-scatter.29
  625.2 39.9 all-gather.49
  667.9 38.5 all-gather.47
  723.8 82.9 reduce-scatter.29
  812.8 21.6 reduce-scatter.23
  837.3 21.8 reduce-scatter.27
  861.9 22.0 reduce-scatter.25
  886.8 22.0 reduce-scatter.17
  911.8 59.9 reduce-scatter.19
  974.8 59.9 reduce-scatter.21
where the time goes:
time: 1360 us; the launch traced here: 1350 us
  waiting for transfers between devices  738 us (54%)
  blocking collectives  423 us (31%)
  local copies, waits for them, and re-layouts  88.5 us (7%)
  matrix products  62.4 us (5%)
  other arithmetic  20 us (1%)
  between operations  19.5 us (1%)
    psum x1, blocking collectives, per_device(): lax.psum((grad_w_query, grad_b_query, grad_w_key, grad_w_value, grad_b_va...  305 us
    while x12, waiting for transfers between devices  160 us
    psum x2, blocking collectives, per_device(): lax.psum((jnp.sum(valid * error * error), jnp.sum(valid)), ('batch', 'ctx'))  78.7 us
    all_gather x2, waiting for transfers between devices, attend_forward(): lax.all_gather(key_one, 'ctx', axis=0, tiled=True)  75.3 us
    all_gather x2, waiting for transfers between devices, attend_backward(): lax.all_gather(value_one, 'ctx', axis=0, tiled=True)  73.7 us
    all_gather x2, waiting for transfers between devices, attend_backward(): lax.all_gather(key_one, 'ctx', axis=0, tiled=True)  73.4 us
    all_gather x2, waiting for transfers between devices, attend_forward(): lax.all_gather(value_one, 'ctx', axis=0, tiled=True)  71.5 us
    reduce_scatter x1, waiting for transfers between devices, per_device(): lax.psum_scatter(grad_w_outer.astype(jnp.bfloat16), 'batch', scatter_dime...  63 us
  transfers between devices with their start and end apart: 22, of which 18 were waited for; matrix products, arithmetic and copies ran while one was open for 6% of the time, Pallas kernels for 0%

commit v1 on v0

--- a/solution.py
+++ b/solution.py
@@ -153,7 +153,7 @@
     valid = (seg_own.reshape(rows_here) != 0).astype(jnp.float32)[:, None]
     error = output - teacher.reshape(rows_here, width)
     loss_total, valid_count = lax.psum(
-        (jnp.sum(valid * error * error), jnp.sum(valid)), ("batch", "ctx")
+        lax.psum((jnp.sum(valid * error * error), jnp.sum(valid)), "batch"), "ctx"
     )
     loss = loss_total / (2.0 * valid_count)
     grad_output = tokens_all / valid_count * valid * error

time: 1360 us -> 1350 us (level)
  blocking collectives: 423 us -> 383 us
  waiting for transfers between devices: 738 us -> 778 us
    psum x3 -> x4, blocking collectives: 383 us -> 344 us  [the longest x2 335 us: per_device(): lax.psum(lax.psum((jnp.sum(valid * error * error), jnp.sum(valid)), 'batc...]
    unnamed x15, waiting for transfers between devices: 4.14 us -> 34.6 us
  transfers between devices with their start and end apart: 22 -> 22, of which waited for: 18 -> 20; matrix products, arithmetic and copies ran while one was open for 6% -> 6% of each run, Pallas kernels for 0% -> 0%
where the time goes in v1:
time: 1350 us
  waiting for transfers between devices  778 us (58%)
  blocking collectives  383 us (28%)
  local copies, waits for them, and re-layouts  88.4 us (7%)
  matrix products  62.4 us (5%)
  other arithmetic  20.1 us (1%)
  between operations  19.4 us (1%)
    psum x2, blocking collectives, per_device(): lax.psum(lax.psum((jnp.sum(valid * error * error), jnp.sum(valid)), 'batc...  335 us
    while x12, waiting for transfers between devices  160 us
    all_gather x2, waiting for transfers between devices, attend_forward(): lax.all_gather(key_one, 'ctx', axis=0, tiled=True)  75.3 us
    all_gather x2, waiting for transfers between devices, attend_backward(): lax.all_gather(value_one, 'ctx', axis=0, tiled=True)  73.7 us
    all_gather x2, waiting for transfers between devices, attend_backward(): lax.all_gather(key_one, 'ctx', axis=0, tiled=True)  73.4 us
    all_gather x2, waiting for transfers between devices, attend_forward(): lax.all_gather(value_one, 'ctx', axis=0, tiled=True)  71.5 us
    reduce_scatter x1, waiting for transfers between devices, per_device(): lax.psum_scatter(grad_w_outer.astype(jnp.bfloat16), 'batch', scatter_dime...  63 us
    reduce_scatter x1, waiting for transfers between devices, per_device(): lax.psum_scatter(grad_w_inner.astype(jnp.bfloat16), 'batch', scatter_dime...  62.9 us
  transfers between devices with their start and end apart: 22, of which 20 were waited for; matrix products, arithmetic and copies ran while one was open for 6% of the time, Pallas kernels for 0%

profile of v1, /device:TPU:1, one launch (start us, length us, event | category | flops | bytes accessed | tf_op | source)
XLA Modules:
  0.0 1352.8 jit_solution(13751252796342598220)
XLA Ops:
  9.5 3.7 all-gather.5
  13.3 3.2 all-gather.4
  17.3 17.2 %all-gather.36.cloned.1.call-done = bf16[768,768]{1,0:T(8,128)(2,1)} async-done(((bf16[384,768]{1,0:T(8,128)(2,1)}), bf16[768,768]{1,0:T(8,128)(2,1)}) %all-gather.36.cloned.1.call-update) | async-done | bytes 1179664 | tf_op jit(solution)/shard_map/all_gather | solution.py:87
  36.8 22.1 %all-gather.34.cloned.1.call-done = bf16[768,768]{1,0:T(8,128)(2,1)} async-done(((bf16[384,768]{1,0:T(8,128)(2,1)}), bf16[768,768]{1,0:T(8,128)(2,1)}) %all-gather.34.cloned.1.call-update) | async-done | bytes 1179664 | tf_op jit(solution)/shard_map/all_gather | solution.py:85
  61.1 22.1 %all-gather.32.cloned.1.call-done = bf16[768,768]{1,0:T(8,128)(2,1)} async-done(((bf16[384,768]{1,0:T(8,128)(2,1)}), bf16[768,768]{1,0:T(8,128)(2,1)}) %all-gather.32.cloned.1.call-update) | async-done | bytes 1179664 | tf_op jit(solution)/shard_map/all_gather | solution.py:88
  85.5 181.2 %while.26 = (s32[]{:T(128)}, bf16[2,64,768]{2,1,0:T(8,128)(2,1)}, f32[2,12,64]{2,1,0:T(8,128)}, bf16[2,64,768]{2,1,0:T(8,128)(2,1)}, s32[2,64]{1,0:T(2,128)S(1)}...) while((s32[]{:T(128)}, bf16[2,64,768]{2,1,0:T(8,128)(2,1)}, ...), condition=%wide.region_3.4_spmd, body=%wide.region_0.3_spmd.sunk | while | flops 210877696 | bytes 30582736 | solution.py:137
  90.6 38.4 %all-gather.46.cloned.1.call-done = bf16[1,1024,768]{2,1,0:T(8,128)(2,1)} async-done(((bf16[1,64,768]{2,1,0:T(8,128)(2,1)}), bf16[1,1024,768]{2,1,0:T(8,128)(2,1)}) %all-gather.46.cloned.1.call-update) | async-done | bytes 1572880 | tf_op jit(solution)/shard_map/while/body/eval_jaxpr/all_gather | solution.py:118
  134.6 35.7 %all-gather.44.cloned.1.call-done = bf16[1,1024,768]{2,1,0:T(8,128)(2,1)} async-done(((bf16[1,64,768]{2,1,0:T(8,128)(2,1)}), bf16[1,1024,768]{2,1,0:T(8,128)(2,1)}) %all-gather.44.cloned.1.call-update) | async-done | bytes 1572880 | tf_op jit(solution)/shard_map/while/body/eval_jaxpr/all_gather | solution.py:119
  181.9 36.9 %all-gather.46.cloned.1.call-done = bf16[1,1024,768]{2,1,0:T(8,128)(2,1)} async-done(((bf16[1,64,768]{2,1,0:T(8,128)(2,1)}), bf16[1,1024,768]{2,1,0:T(8,128)(2,1)}) %all-gather.46.cloned.1.call-update) | async-done | bytes 1572880 | tf_op jit(solution)/shard_map/while/body/eval_jaxpr/all_gather | solution.py:118
  224.4 35.8 %all-gather.44.cloned.1.call-done = bf16[1,1024,768]{2,1,0:T(8,128)(2,1)} async-done(((bf16[1,64,768]{2,1,0:T(8,128)(2,1)}), bf16[1,1024,768]{2,1,0:T(8,128)(2,1)}) %all-gather.44.cloned.1.call-update) | async-done | bytes 1572880 | tf_op jit(solution)/shard_map/while/body/eval_jaxpr/all_gather | solution.py:119
  260.2 2.6 copy.121
  269.4 4.4 psum.135
  273.9 30.8 %psum.136 = f32[]{:T(128)} all-reduce(f32[]{:T(128)} %psum.135), channel_id=1, replica_groups=mesh['batch'=2,'ctx'=16] {'ctx'}, use_global_device_ids=true, to_apply=%region_13.14 | all-reduce | flops 1 | bytes 8 | tf_op jit(solution)/shard_map/psum | solution.py:155
  304.7 3.5 all-gather.6
  308.3 3.5 all-gather.7
  311.8 3.5 all-gather.8
  315.4 3.5 all-gather.10
  319.0 3.5 all-gather.11
  322.5 3.5 all-gather.12
  327.0 3.8 all-gather.9
  332.8 22.1 %all-gather.40.cloned.1.call-done = bf16[768,3072]{1,0:T(8,128)(2,1)} async-done(((bf16[384,3072]{1,0:T(8,128)(2,1)}), bf16[768,3072]{1,0:T(8,128)(2,1)}) %all-gather.40.cloned.1.call-update) | async-done | bytes 4718608 | tf_op jit(solution)/shard_map/all_gather | solution.py:94
  354.9 7.6 multiply_convert_fusion.1
  362.5 56.5 %all-gather.42.cloned.1.call-done = bf16[3072,768]{1,0:T(8,128)(2,1)} async-done(((bf16[1536,768]{1,0:T(8,128)(2,1)}), bf16[3072,768]{1,0:T(8,128)(2,1)}) %all-gather.42.cloned.1.call-update) | async-done | bytes 4718608 | tf_op jit(solution)/shard_map/all_gather | solution.py:96
  419.0 3.4 fusion.45
  433.1 376.0 %while.27 = (s32[]{:T(128)}, bf16[2,64,768]{1,2,0:T(8,128)(2,1)}, bf16[2,64,768]{1,2,0:T(8,128)(2,1)}, bf16[2,64,768]{1,2,0:T(8,128)(2,1)}, bf16[2,64,768]{2,1,0...) while((s32[]{:T(128)}, bf16[2,64,768]{1,2,0:T(8,128)(2,1)}, ...), condition=%wide.region_21.22_spmd, body=%wide.region_18.21_spmd.sunk | while | flops 512916736 | bytes 120094944 | solution.py:229
  439.9 37.1 %all-gather.50.cloned.1.call-done = bf16[1,1024,768]{2,1,0:T(8,128)(2,1)} async-done(((bf16[1,64,768]{2,1,0:T(8,128)(2,1)}), bf16[1,1024,768]{2,1,0:T(8,128)(2,1)}) %all-gather.50.cloned.1.call-update) | async-done | bytes 1572880 | tf_op jit(solution)/shard_map/while/body/eval_jaxpr/all_gather | solution.py:183
  481.5 36.7 %all-gather.48.cloned.1.call-done = bf16[1,1024,768]{2,1,0:T(8,128)(2,1)} async-done(((bf16[1,64,768]{2,1,0:T(8,128)(2,1)}), bf16[1,1024,768]{2,1,0:T(8,128)(2,1)}) %all-gather.48.cloned.1.call-update) | async-done | bytes 1572880 | tf_op jit(solution)/shard_map/while/body/eval_jaxpr/all_gather | solution.py:182
  520.8 2.8 multiply_reduce_fusion.9
  525.7 3.2 pad_maximum_fusion.2
  528.9 6.6 copy.128
  538.6 80.0 %reduce-scatter.30.cloned.1.call-done = f32[64,1536]{1,0:T(8,128)} async-done(((f32[1024,1536]{1,0:T(8,128)}), f32[64,1536]{1,0:T(8,128)}) %reduce-scatter.30.cloned.1.call-update) | async-done | bytes 393232 | tf_op jit(solution)/shard_map/while
  628.1 36.6 %all-gather.50.cloned.1.call-done = bf16[1,1024,768]{2,1,0:T(8,128)(2,1)} async-done(((bf16[1,64,768]{2,1,0:T(8,128)(2,1)}), bf16[1,1024,768]{2,1,0:T(8,128)(2,1)}) %all-gather.50.cloned.1.call-update) | async-done | bytes 1572880 | tf_op jit(solution)/shard_map/while/body/eval_jaxpr/all_gather | solution.py:183
  669.3 36.7 %all-gather.48.cloned.1.call-done = bf16[1,1024,768]{2,1,0:T(8,128)(2,1)} async-done(((bf16[1,64,768]{2,1,0:T(8,128)(2,1)}), bf16[1,1024,768]{2,1,0:T(8,128)(2,1)}) %all-gather.48.cloned.1.call-update) | async-done | bytes 1572880 | tf_op jit(solution)/shard_map/while/body/eval_jaxpr/all_gather | solution.py:182
  708.6 2.8 multiply_reduce_fusion.9
  713.4 3.2 pad_maximum_fusion.2
  716.6 6.6 copy.128
  726.4 80.0 %reduce-scatter.30.cloned.1.call-done = f32[64,1536]{1,0:T(8,128)} async-done(((f32[1024,1536]{1,0:T(8,128)}), f32[64,1536]{1,0:T(8,128)}) %reduce-scatter.30.cloned.1.call-update) | async-done | bytes 393232 | tf_op jit(solution)/shard_map/while
  818.2 3.7 convolution_convert_fusion.1
  823.0 3.6 convolution_convert_fusion
  829.8 4.3 psum.133
  838.9 7.3 all-reduce.10
  851.7 7.3 reduce-scatter.28.cloned.1.call-done
  860.4 23.2 %reduce-scatter.26.cloned.1.call-done = bf16[384,768]{1,0:T(8,128)(2,1)} async-done(((bf16[768,768]{1,0:T(8,128)(2,1)}), bf16[384,768]{1,0:T(8,128)(2,1)}) %reduce-scatter.26.cloned.1.call-update) | async-done | bytes 589840
  885.0 23.2 %reduce-scatter.18.cloned.1.call-done = bf16[384,768]{1,0:T(8,128)(2,1)} async-done(((bf16[768,768]{1,0:T(8,128)(2,1)}), bf16[384,768]{1,0:T(8,128)(2,1)}) %reduce-scatter.18.cloned.1.call-update) | async-done | bytes 589840 | tf_op jit(solution)/shard_map/reduce_scatter | solution.py:279
  908.2 62.9 %reduce-scatter.20.cloned.1.call-done = bf16[384,3072]{1,0:T(8,128)(2,1)} async-done(((bf16[768,3072]{1,0:T(8,128)(2,1)}), bf16[384,3072]{1,0:T(8,128)(2,1)}) %reduce-scatter.20.cloned.1.call-update) | async-done | bytes 2359312 | tf_op jit(solution)/shard_map/reduce_scatter | solution.py:291
  971.1 63.0 %reduce-scatter.22.cloned.1.call-done = bf16[1536,768]{1,0:T(8,128)(2,1)} async-done(((bf16[3072,768]{1,0:T(8,128)(2,1)}), bf16[1536,768]{1,0:T(8,128)(2,1)}) %reduce-scatter.22.cloned.1.call-update) | async-done | bytes 2359312 | tf_op jit(solution)/shard_map/reduce_scatter | solution.py:297
  1034.1 304.6 %all-reduce.12 = (f32[]{:T(128)}, f32[384,768]{0,1:T(8,128)}, f32[384]{0:T(512)}, f32[384,768]{0,1:T(8,128)}, f32[384,768]{0,1:T(8,128)S(1)}, /*index=5*/f32[384...) all-reduce(f32[]{:T(128)} %psum.133, ...), channel_id=1, replica_groups=mesh['batch'=2,'ctx'=16] {'ctx'}, use_global_device_ids=true, to_apply=%region_10.11 | all-reduce | flops 3543553 | bytes 21270536 | tf_op jit(solution)/shard_map/psum | solution.py:155
  1338.7 2.7 copy.83
  (325 shorter events, 127.5 us)
Async XLA Ops:
  7.2 10.0 copy-start.5
  7.2 27.3 %all-gather.36.cloned.1.call-start = ((), (), s32[]{:S(2)}) async-start(), calls=%async_computation.9 | async-start | bytes 1769472 | tf_op jit(solution)/shard_map/all_gather | solution.py:87
  8.0 50.9 %all-gather.34.cloned.1.call-start = ((), (), s32[]{:S(2)}) async-start(), calls=%async_computation.8 | async-start | bytes 1769472 | tf_op jit(solution)/shard_map/all_gather | solution.py:85
  8.7 74.5 %all-gather.32.cloned.1.call-start = ((), (), s32[]{:S(2)}) async-start(), calls=%async_computation.7 | async-start | bytes 1769472 | tf_op jit(solution)/shard_map/all_gather | solution.py:88
  85.5 43.5 %all-gather.46.cloned.1.call-start = ((), (), s32[]{:S(2)}) async-start(), calls=%async_computation.20 | async-start | bytes 1671168 | tf_op jit(solution)/shard_map/while/body/eval_jaxpr/all_gather | solution.py:118
  87.1 83.2 %all-gather.44.cloned.1.call-start = ((), (), s32[]{:S(2)}) async-start(), calls=%async_computation.19 | async-start | bytes 1671168 | tf_op jit(solution)/shard_map/while/body/eval_jaxpr/all_gather | solution.py:119
  176.8 42.0 %all-gather.46.cloned.1.call-start = ((), (), s32[]{:S(2)}) async-start(), calls=%async_computation.20 | async-start | bytes 1671168 | tf_op jit(solution)/shard_map/while/body/eval_jaxpr/all_gather | solution.py:118
  178.3 81.8 %all-gather.44.cloned.1.call-start = ((), (), s32[]{:S(2)}) async-start(), calls=%async_computation.19 | async-start | bytes 1671168 | tf_op jit(solution)/shard_map/while/body/eval_jaxpr/all_gather | solution.py:119
  266.7 64.1 %all-gather.38.cloned.1.call-start = ((), (), s32[]{:S(2)}) async-start(), calls=%async_computation.10 | async-start | bytes 1769472 | tf_op jit(solution)/shard_map/all_gather | solution.py:90
  267.4 87.5 %all-gather.40.cloned.1.call-start = ((), (), s32[]{:S(2)}) async-start(), calls=%async_computation.11 | async-start | bytes 7077888 | tf_op jit(solution)/shard_map/all_gather | solution.py:94
  268.2 36.6 %copy-start.46 = (bf16[384]{0:T(512)(128)(2,1)S(1)}, bf16[384]{0:T(512)(128)(2,1)}, u32[]{:S(2)}) copy-start(bf16[384]{0:T(512)(128)(2,1)} %param.31) | copy-start | bytes 2308
  268.2 40.1 %copy-start.47 = (bf16[384]{0:T(512)(128)(2,1)S(1)}, bf16[384]{0:T(512)(128)(2,1)}, u32[]{:S(2)}) copy-start(bf16[384]{0:T(512)(128)(2,1)} %param.32) | copy-start | bytes 2308
  268.2 43.6 %copy-start.48 = (bf16[384]{0:T(512)(128)(2,1)S(1)}, bf16[384]{0:T(512)(128)(2,1)}, u32[]{:S(2)}) copy-start(bf16[384]{0:T(512)(128)(2,1)} %param.33) | copy-start | bytes 2308
  268.2 47.2 %copy-start.49 = (bf16[384]{0:T(512)(128)(2,1)S(1)}, bf16[384]{0:T(512)(128)(2,1)}, u32[]{:S(2)}) copy-start(bf16[384]{0:T(512)(128)(2,1)} %param.37) | copy-start | bytes 2308
  268.2 50.8 %copy-start.50 = (bf16[384]{0:T(512)(128)(2,1)S(1)}, bf16[384]{0:T(512)(128)(2,1)}, u32[]{:S(2)}) copy-start(bf16[384]{0:T(512)(128)(2,1)} %param.38) | copy-start | bytes 2308
  268.2 54.3 %copy-start.51 = (bf16[384]{0:T(512)(128)(2,1)S(1)}, bf16[384]{0:T(512)(128)(2,1)}, u32[]{:S(2)}) copy-start(bf16[384]{0:T(512)(128)(2,1)} %param.39) | copy-start | bytes 2308
  268.2 58.7 %copy-start.42 = (bf16[1536]{0:T(1024)(128)(2,1)S(1)}, bf16[1536]{0:T(1024)(128)(2,1)}, u32[]{:S(2)}) copy-start(bf16[1536]{0:T(1024)(128)(2,1)} %param.35) | copy-start | bytes 9220
  268.2 62.6 %copy-start.6 = (f32[2,64,768]{2,1,0:T(8,128)S(1)}, f32[2,64,768]{2,1,0:T(8,128)}, u32[]{:S(2)}) copy-start(f32[2,64,768]{2,1,0:T(8,128)} %param.22) | copy-start | bytes 1179652
  268.2 62.6 %copy-start.26 = (bf16[2,64,768]{2,1,0:T(8,128)(2,1)S(1)}, bf16[2,64,768]{2,1,0:T(8,128)(2,1)}, u32[]{:S(2)}) copy-start(bf16[2,64,768]{2,1,0:T(8,128)(2,1)} %get-tuple-element.120) | copy-start | bytes 589828
  268.3 150.7 %all-gather.42.cloned.1.call-start = ((), (), s32[]{:S(2)}) async-start(), calls=%async_computation.12 | async-start | bytes 7077888 | tf_op jit(solution)/shard_map/all_gather | solution.py:96
  332.5 97.6 %copy-start.3 = (f32[128,768]{1,0:T(8,128)}, f32[128,768]{1,0:T(8,128)S(1)}, u32[]{:S(2)}) copy-start(f32[128,768]{1,0:T(8,128)S(1)} %get-tuple-element.312) | copy-start | bytes 1179652
  332.6 97.6 %copy-start.32 = (f32[128]{0:T(128)}, f32[128]{0:T(128)S(1)}, u32[]{:S(2)}) copy-start(f32[128]{0:T(128)S(1)} %broadcast_multiply_fusion.1) | copy-start | bytes 1540
  332.8 97.4 %copy-start.34 = (f32[128]{0:T(128)}, f32[128]{0:T(128)S(1)}, u32[]{:S(2)}) copy-start(f32[128]{0:T(128)S(1)} %fusion.30) | copy-start | bytes 1540
  362.5 59.9 %copy-start.8 = (bf16[128,3072]{1,0:T(8,128)(2,1)}, bf16[128,3072]{1,0:T(8,128)(2,1)S(1)}, u32[]{:S(2)}) copy-start(bf16[128,3072]{1,0:T(8,128)(2,1)S(1)} %get-tuple-element.301) | copy-start | bytes 2359300
  433.1 43.8 %all-gather.50.cloned.1.call-start = ((), (), s32[]{:S(2)}) async-start(), calls=%async_computation.22 | async-start | bytes 1671168 | tf_op jit(solution)/shard_map/while/body/eval_jaxpr/all_gather | solution.py:183
  434.7 83.5 %all-gather.48.cloned.1.call-start = ((), (), s32[]{:S(2)}) async-start(), calls=%async_computation.21 | async-start | bytes 1671168 | tf_op jit(solution)/shard_map/while/body/eval_jaxpr/all_gather | solution.py:182
  436.3 182.3 %reduce-scatter.30.cloned.1.call-start = ((), (), s32[]{:S(2)}) async-start(), calls=%async_computation.23 | async-start | bytes 6684672 | tf_op jit(solution)/shard_map/while
  537.3 82.5 %copy-start.17 = (bf16[2,64,768]{1,2,0:T(8,128)(2,1)S(1)}, bf16[2,64,768]{1,2,0:T(8,128)(2,1)}, u32[]{:S(2)}) copy-start(bf16[2,64,768]{1,2,0:T(8,128)(2,1)} %get-tuple-element.499) | copy-start | bytes 589828 | tf_op jit(solution)/shard_map/while
  537.9 83.4 %copy-start.41 = (s32[2,64]{1,0:T(2,128)S(1)}, s32[2,64]{1,0:T(2,128)}, u32[]{:S(2)}) copy-start(s32[2,64]{1,0:T(2,128)} %copy-done.40) | copy-start | bytes 1540 | tf_op jit(solution)/shard_map/while
  621.3 43.4 %all-gather.50.cloned.1.call-start = ((), (), s32[]{:S(2)}) async-start(), calls=%async_computation.22 | async-start | bytes 1671168 | tf_op jit(solution)/shard_map/while/body/eval_jaxpr/all_gather | solution.py:183
  622.9 83.1 %all-gather.48.cloned.1.call-start = ((), (), s32[]{:S(2)}) async-start(), calls=%async_computation.21 | async-start | bytes 1671168 | tf_op jit(solution)/shard_map/while/body/eval_jaxpr/all_gather | solution.py:182
  624.5 181.9 %reduce-scatter.30.cloned.1.call-start = ((), (), s32[]{:S(2)}) async-start(), calls=%async_computation.23 | async-start | bytes 6684672 | tf_op jit(solution)/shard_map/while
  725.1 82.5 %copy-start.17 = (bf16[2,64,768]{1,2,0:T(8,128)(2,1)S(1)}, bf16[2,64,768]{1,2,0:T(8,128)(2,1)}, u32[]{:S(2)}) copy-start(bf16[2,64,768]{1,2,0:T(8,128)(2,1)} %get-tuple-element.499) | copy-start | bytes 589828 | tf_op jit(solution)/shard_map/while
  725.7 83.4 %copy-start.41 = (s32[2,64]{1,0:T(2,128)S(1)}, s32[2,64]{1,0:T(2,128)}, u32[]{:S(2)}) copy-start(s32[2,64]{1,0:T(2,128)} %copy-done.40) | copy-start | bytes 1540 | tf_op jit(solution)/shard_map/while
  809.1 41.3 %reduce-scatter.24.cloned.1.call-start = ((), (), s32[]{:S(2)}) async-start(), calls=%async_computation.16 | async-start | bytes 1769472
  812.2 46.8 %reduce-scatter.28.cloned.1.call-start = ((), (), s32[]{:S(2)}) async-start(), calls=%async_computation.18 | async-start | bytes 1769472
  814.3 69.3 %reduce-scatter.26.cloned.1.call-start = ((), (), s32[]{:S(2)}) async-start(), calls=%async_computation.17 | async-start | bytes 1769472
  816.5 91.7 %reduce-scatter.18.cloned.1.call-start = ((), (), s32[]{:S(2)}) async-start(), calls=%async_computation.13 | async-start | bytes 1769472 | tf_op jit(solution)/shard_map/reduce_scatter | solution.py:279
  818.1 153.0 %reduce-scatter.20.cloned.1.call-start = ((), (), s32[]{:S(2)}) async-start(), calls=%async_computation.14 | async-start | bytes 7077888 | tf_op jit(solution)/shard_map/reduce_scatter | solution.py:291
  821.9 212.2 %reduce-scatter.22.cloned.1.call-start = ((), (), s32[]{:S(2)}) async-start(), calls=%async_computation.15 | async-start | bytes 7077888 | tf_op jit(solution)/shard_map/reduce_scatter | solution.py:297
  826.6 12.2 copy-start.36
  826.7 12.2 copy-start.37
  826.7 12.2 copy-start.38
  826.7 12.2 copy-start.39
  826.7 19.9 %copy-start.13 = (bf16[768,768]{1,0:T(8,128)(2,1)S(1)}, bf16[768,768]{1,0:T(8,128)(2,1)}, u32[]{:S(2)}) copy-start(bf16[768,768]{1,0:T(8,128)(2,1)} %all-gather.34.cloned.1.call-done) | copy-start | bytes 3538948
  826.7 19.9 %copy-start.16 = (f32[128,768]{1,0:T(8,128)S(1)}, f32[128,768]{1,0:T(8,128)}, u32[]{:S(2)}) copy-start(f32[128,768]{1,0:T(8,128)} %copy-done.15) | copy-start | bytes 1179652
  837.5 10.4 copy-start.11
  837.5 10.4 copy-start.28
  (37 other events, 80.7 us)
Sparse Core Ops, SparseCore 0:
  9.6 24.8 all-gather.35
  36.0 22.7 all-gather.33
  60.4 22.7 all-gather.31
  88.9 40.0 all-gather.45
  131.7 38.5 all-gather.43
  180.1 38.5 all-gather.45
  221.6 38.5 all-gather.43
  269.0 21.2 all-gather.37
  291.9 62.9 all-gather.39
  356.3 62.6 all-gather.41
  436.8 40.1 all-gather.49
  479.6 38.5 all-gather.47
  535.6 82.9 reduce-scatter.29
  624.7 39.9 all-gather.49
  667.4 38.5 all-gather.47
  723.4 82.9 reduce-scatter.29
  812.4 21.5 reduce-scatter.23
  836.8 22.1 reduce-scatter.27
  861.9 21.7 reduce-scatter.25
  886.4 21.7 reduce-scatter.17
  911.0 59.9 reduce-scatter.19
  974.1 59.9 reduce-scatter.21
